TPU v7x, 256 devices: a whole 4x4x8 slice. The times are simulated.
256 devices in a mesh: node: 64 (over z, x, core), site: 4 (over y).
Axes of the slice: x: 4, y: 4, z: 8, core: 2. Of those that a mesh axis runs over, the one named last changes fastest.
Arguments:
- leaf_partials: float32 [4096, 4, 4096], P('node', None, 'site'), may hold values from 0.05 to 1
- dag_edges: int32 [3, 12288, 3], P(None, 'node'), may hold values from 0 to 4095, as said below
- weights: float32 [3, 12288], P(None, 'node'), may hold values from 0.25 to 4
- lengths: float32 [3, 12288], P(None, 'node'), may hold values from 0.02 to 2
- counts: int32 [4096], P('site'), may hold values from 1 to 9
- topo_nodes: int32 [256, 8], P('node'), may hold values from 0 to 4095
Outputs:
- topology_loglik: float32 [256], P('node')
- edge_gradient: float32 [12288], P('node')
Inputs may be any that keep to these rules, and one draw needn't show every extreme that they name: `dag_edges`: in every level each subsplit is the child of exactly 3 edges, listed on the index of node that owns the child; subsplit n is owned by index n // 64. Column 1 is the parent in the next level, column 2 the rotation (0 or 1). Every parent has at least one edge of each rotation. Among the edges of one index of node, at most 4 have parents owned by any one index, and some index receives exactly 4 from every index.
All inputs are finite; a program needn't handle non-finite values.
Results may differ from a plain program's by a relative error of at most 0.0003.
Values sent between devices are 32-bit elements; how exact they have to be, the bound alone decides.
No kernel may reach another device: no remote copies, remote signals or barrier semaphores. Data moves between devices by JAX's collectives and lax.ppermute only.
A program may use at most 192 MiB of HBM per device.

v0:
```python
import jax
import jax.numpy as jnp
from jax import lax
from jax.sharding import PartitionSpec as P


def transit(child_rows, branch):
    survival = jnp.exp(branch * (-4.0 / 3.0))[:, None, None]
    return survival * child_rows + (1.0 - survival) * 0.25 * jnp.sum(
        child_rows, axis=1, keepdims=True
    )


def on_device(leaf_partials, dag_edges, weights, lengths, counts, topo_nodes):
    node_dev, states, site_dev = leaf_partials.shape
    level_count, edge_dev = (dag_edges.shape[0], dag_edges.shape[1])
    owners = lax.axis_size("node")
    device = lax.axis_index("node")
    nodes_all = node_dev * owners
    sites_all = site_dev * lax.axis_size("site")
    scaled = counts.astype(jnp.float32) / sites_all
    incidence = lax.all_gather(topo_nodes, "node", axis=0, tiled=True)
    multiplicity = jax.ops.segment_sum(
        jnp.ones((incidence.size,), jnp.float32), incidence.reshape(-1), num_segments=nodes_all
    )
    capacity = 4 * node_dev // owners
    slots_all = owners * capacity
    current = leaf_partials
    for level_index in range(level_count):
        child_index = dag_edges[level_index, :, 0] - device * node_dev
        parents = dag_edges[level_index, :, 1]
        rotation = dag_edges[level_index, :, 2]
        message = transit(current[child_index], lengths[level_index])
        owner_dev = parents // node_dev
        one_hot = (owner_dev[:, None] == jnp.arange(owners)[None, :]).astype(jnp.int32)
        slot_rank = jnp.sum((jnp.cumsum(one_hot, axis=0) - one_hot) * one_hot, axis=1)
        slot_index = owner_dev * capacity + slot_rank
        pair_code = ((parents - owner_dev * node_dev) * 2 + rotation).astype(jnp.float32)
        buffer = jnp.zeros((slots_all, states, site_dev), jnp.float32).at[slot_index].set(message)
        code_buffer = jnp.full((slots_all,), -1.0, jnp.float32).at[slot_index].set(pair_code)
        weight_buffer = (
            jnp.zeros((slots_all,), jnp.float32).at[slot_index].set(weights[level_index])
        )
        received, received_codes, received_weights = (
            lax.all_to_all(
                buffer.reshape(owners, capacity, states, site_dev),
                "node",
                split_axis=0,
                concat_axis=0,
                tiled=True,
            ),
            lax.all_to_all(
                code_buffer.reshape(owners, capacity),
                "node",
                split_axis=0,
                concat_axis=0,
                tiled=True,
            ),
            lax.all_to_all(
                weight_buffer.reshape(owners, capacity),
                "node",
                split_axis=0,
                concat_axis=0,
                tiled=True,
            ),
        )
        flat_rows = received.reshape(slots_all, states * site_dev)
        selector = (
            received_codes.reshape(-1).astype(jnp.int32)[None, :]
            == jnp.arange(2 * node_dev)[:, None]
        ).astype(jnp.float32)
        summed = jnp.dot(
            selector * received_weights.reshape(-1)[None, :],
            flat_rows,
            precision=lax.Precision.HIGHEST,
            preferred_element_type=jnp.float32,
        )
        pair_sums = summed.reshape(node_dev, 2, states, site_dev)
        current = pair_sums[:, 0] * pair_sums[:, 1]
    denominator = 0.25 * jnp.sum(current, axis=1)
    node_part = jnp.sum(scaled[None, :] * jnp.log(denominator), axis=1)
    adjoint = pair_sums[:, ::-1] * (scaled[None, :] * 0.25 / denominator)[:, None, None, :]
    adjoint_slots = jnp.dot(
        selector.T,
        adjoint.reshape(2 * node_dev, states * site_dev),
        precision=lax.Precision.HIGHEST,
        preferred_element_type=jnp.float32,
    )
    grad_part = jnp.sum(flat_rows * adjoint_slots, axis=1)
    node_scores, slot_grads = lax.psum((node_part, grad_part), "site")
    own_mult = lax.dynamic_slice_in_dim(multiplicity, device * node_dev, node_dev)
    pair_mult = jnp.repeat(own_mult, 2)
    slot_mult = jnp.dot(
        selector.T, pair_mult, precision=lax.Precision.HIGHEST, preferred_element_type=jnp.float32
    )
    returned = lax.all_to_all(
        (slot_grads * slot_mult).reshape(owners, capacity),
        "node",
        split_axis=0,
        concat_axis=0,
        tiled=True,
    )
    edge_gradient = returned.reshape(-1)[slot_index]
    score_table = lax.all_gather(node_scores, "node", axis=0, tiled=True)
    topology_loglik = jnp.sum(score_table[topo_nodes], axis=1)
    return (topology_loglik, edge_gradient)


def solution(mesh):
    return jax.shard_map(
        on_device,
        mesh=mesh,
        in_specs=(
            P("node", None, "site"),
            P(None, "node", None),
            P(None, "node"),
            P(None, "node"),
            P("site"),
            P("node", None),
        ),
        out_specs=(P("node"), P("node")),
        check_vma=False,
    )
```

profile of v0, /device:TPU:0, one launch (start us, length us, event | category | flops | bytes accessed | tf_op | source)
XLA Modules:
  0.0 903.7 jit_solution(11495351797183941422)
XLA Ops:
  0.6 0.9 fusion.54
  4.6 0.8 compare_select_fusion
  5.4 1.2 scatter_custom_fusion.4
  6.6 0.7 all_to_all.59
  7.3 10.2 %all-to-all-start.4 = ((f32[64,1,4]{2,1,0:T(1,128)}), f32[64,1,4]{2,1,0:T(1,128)S(1)}, u32[]{:S(2)}, u32[]{:S(2)}) async-start(f32[64,1,4]{2,1,0:T(1,128)} %bitcast.30), calls=%async_computation.4 | async-start | bytes 65536 | tf_op jit(solution)/shard_map/all_to_all | solution.py:52
  17.6 0.8 multiply_exponential_fusion.2
  18.4 4.1 gather_fusion
  22.5 3.8 reduce_sum.102
  26.4 1.2 scatter_custom_fusion.5
  27.6 0.7 all_to_all.61
  28.3 10.3 %all-to-all-start.5 = ((f32[64,1,4]{2,1,0:T(1,128)}), f32[64,1,4]{2,1,0:T(1,128)S(1)}, u32[]{:S(2)}, u32[]{:S(2)}) async-start(f32[64,1,4]{2,1,0:T(1,128)} %bitcast.32), calls=%async_computation.5 | async-start | bytes 65536 | tf_op jit(solution)/shard_map/all_to_all | solution.py:59
  38.6 3.8 multiply_add_fusion.2
  42.4 3.0 broadcast.594.clone.1
  45.5 26.2 %scatter_fusion = f32[256,4,1024]{2,1,0:T(4,128)} fusion(f32[256,4,1024]{2,1,0:T(4,128)} %broadcast.594.clone.1, s32[192]{0:T(256)S(1)} %bitcast.186, f32[192,4,1024]{2,1,0:T(4,128)} %multiply_add_fusion.2), kind=kCustom, calls=%fused_computation.11 | custom fusion | bytes 9437952 | tf_op jit(solution)/shard_map/scatter | solution.py:39
  71.6 10.7 %all-to-all-start.6 = ((f32[64,4,4,1024]{3,2,1,0:T(4,128)}), f32[64,4,4,1024]{3,2,1,0:T(4,128)}, u32[]{:S(2)}, u32[]{:S(2)}) async-start(f32[64,4,4,1024]{3,2,1,0:T(4,128)} %bitcast.159), calls=%async_computation.6 | async-start | bytes 8388608 | tf_op jit(solution)/shard_map/all_to_all | solution.py:45
  82.4 1.2 scatter_custom_fusion.2
  83.6 0.7 all_to_all.55
  84.3 1.2 scatter_custom_fusion.3
  85.5 0.7 all_to_all.57
  86.9 0.7 reduce.35
  87.8 90.8 %all-to-all-done.6 = f32[64,4,4,1024]{3,2,1,0:T(4,128)} async-done(((f32[64,4,4,1024]{3,2,1,0:T(4,128)}), f32[64,4,4,1024]{3,2,1,0:T(4,128)}, u32[]{:S(2)}, u32[]{:S(2)}) %all-to-all-start.6) | async-done | bytes 4194336 | tf_op jit(solution)/shard_map/all_to_all | solution.py:45
  178.6 5.3 all-to-all-start.2
  183.8 8.0 copy.51
  191.8 5.8 copy.35
  197.6 6.6 fusion.4
  205.0 4.1 gather_fusion.1
  209.1 3.8 reduce_sum.103
  213.0 10.3 %all-to-all-start.3 = ((f32[64,1,4]{2,1,0:T(1,128)}), f32[64,1,4]{2,1,0:T(1,128)S(1)}, u32[]{:S(2)}, u32[]{:S(2)}) async-start(f32[64,1,4]{2,1,0:T(1,128)} %bitcast.20), calls=%async_computation.3 | async-start | bytes 65536 | tf_op jit(solution)/shard_map/all_to_all | solution.py:59
  223.3 3.8 multiply_add_fusion.1
  227.1 3.0 broadcast.594.clone
  230.1 26.2 %scatter_fusion.1 = f32[256,4,1024]{2,1,0:T(4,128)} fusion(f32[256,4,1024]{2,1,0:T(4,128)} %broadcast.594.clone, s32[192]{0:T(256)S(1)} %bitcast.182, f32[192,4,1024]{2,1,0:T(4,128)} %multiply_add_fusion.1), kind=kCustom, calls=%fused_computation.12 | custom fusion | bytes 9437952 | tf_op jit(solution)/shard_map/scatter | solution.py:39
  256.3 10.9 %all-to-all-start.7 = ((f32[64,4,4,1024]{3,2,1,0:T(4,128)}), f32[64,4,4,1024]{3,2,1,0:T(4,128)}, u32[]{:S(2)}, u32[]{:S(2)}) async-start(f32[64,4,4,1024]{3,2,1,0:T(4,128)} %bitcast.160), calls=%async_computation.7 | async-start | bytes 8388608 | tf_op jit(solution)/shard_map/all_to_all | solution.py:45
  267.3 1.2 scatter_custom_fusion
  268.5 0.7 all_to_all.51
  269.2 1.2 scatter_custom_fusion.1
  270.4 0.7 all_to_all.53
  271.3 0.7 reduce.36
  272.2 91.3 %all-to-all-done.7 = f32[64,4,4,1024]{3,2,1,0:T(4,128)} async-done(((f32[64,4,4,1024]{3,2,1,0:T(4,128)}), f32[64,4,4,1024]{3,2,1,0:T(4,128)}, u32[]{:S(2)}, u32[]{:S(2)}) %all-to-all-start.7) | async-done | bytes 4194336 | tf_op jit(solution)/shard_map/all_to_all | solution.py:45
  363.5 5.3 all-to-all-start
  368.7 8.0 copy.52
  376.7 5.7 copy.37
  382.4 6.6 fusion.6
  389.9 4.1 gather_fusion.2
  393.9 3.8 reduce_sum.104
  397.9 10.3 %all-to-all-start.1 = ((f32[64,1,4]{2,1,0:T(1,128)}), f32[64,1,4]{2,1,0:T(1,128)S(1)}, u32[]{:S(2)}, u32[]{:S(2)}) async-start(f32[64,1,4]{2,1,0:T(1,128)} %bitcast.8), calls=%async_computation.1 | async-start | bytes 65536 | tf_op jit(solution)/shard_map/all_to_all | solution.py:59
  408.2 3.8 multiply_add_fusion
  412.0 3.0 broadcast.594
  415.0 26.2 %scatter_fusion.2 = f32[256,4,1024]{2,1,0:T(4,128)} fusion(f32[256,4,1024]{2,1,0:T(4,128)} %broadcast.594, s32[192]{0:T(256)S(1)} %bitcast.171, f32[192,4,1024]{2,1,0:T(4,128)} %multiply_add_fusion), kind=kCustom, calls=%fused_computation.13 | custom fusion | bytes 9437952 | tf_op jit(solution)/shard_map/scatter | solution.py:39
  441.2 10.7 %all-to-all-start.8 = ((f32[64,4,4,1024]{3,2,1,0:T(4,128)}), f32[64,4,4,1024]{3,2,1,0:T(4,128)}, u32[]{:S(2)}, u32[]{:S(2)}) async-start(f32[64,4,4,1024]{3,2,1,0:T(4,128)} %bitcast.161), calls=%async_computation.8 | async-start | bytes 8388608 | tf_op jit(solution)/shard_map/all_to_all | solution.py:45
  451.9 135.2 %all-gather = s32[64,4,8]{2,1,0:T(4,128)S(1)} all-gather(s32[1,4,8]{2,1,0:T(4,128)S(1)} %bitcast.179), channel_id=1, replica_groups=mesh['node'=64,'site'=4] {'node'}, dimensions={0}, use_global_device_ids=true | all-gather | bytes 8320 | tf_op jit(solution)/shard_map/all_gather | solution.py:22
  587.3 11.2 %scatter_custom_fusion.9 = f32[4096]{0:T(1024)S(1)} fusion(s32[2048]{0:T(1024)S(1)} %reshape.800, f32[2048]{0:T(1024)S(1)} %broadcast.600, f32[]{:T(128)} %constant.79.clone.1), kind=kCustom, calls=%fused_computation.94 | custom fusion | flops 2048 | bytes 16388 | tf_op jit(solution)/shard_map/scatter-add | solution.py:23
  600.4 0.7 reduce.37
  601.5 8.0 copy.53
  609.4 5.6 copy.39
  615.0 6.6 fusion.8
  622.3 1.4 copy.40
  623.6 1.7 copy.54
  625.8 2.4 fusion
  628.2 10.7 %all-reduce.4 = (f32[64]{0:T(128)S(1)}, f32[256]{0:T(256)S(1)}) all-reduce(f32[64]{0:T(128)S(1)} %get-tuple-element.11, f32[256]{0:T(256)S(1)} %fusion), channel_id=1, replica_groups=mesh['node'=64,'site'=4] {'site'}, use_global_device_ids=true, to_apply=%region_23.24 | all-reduce | flops 320 | bytes 2560 | tf_op jit(solution)/shard_map/psum | solution.py:90
  639.0 0.7 all_to_all.66
  639.7 7.9 all-to-all-start.9
  647.8 251.0 %all-reduce.3 = f32[4096]{0:T(1024)S(1)} all-reduce(f32[4096]{0:T(1024)S(1)} %dynamic-update-slice), channel_id=1, replica_groups=mesh['node'=64,'site'=4] {'node'}, use_global_device_ids=true, to_apply=%add.3 | all-reduce | flops 4096 | bytes 32768
  900.3 0.7 reduce.38
  901.1 2.2 gather_fusion.4
  (96 shorter events, 10.8 us)
Async XLA Ops:
  0.6 17.8 %copy-start = (f32[64,4,1024]{2,1,0:T(4,128)S(1)}, f32[64,4,1024]{2,1,0:T(4,128)}, u32[]{:S(2)}) copy-start(f32[64,4,1024]{2,1,0:T(4,128)} %param.6) | copy-start | bytes 3145732
  7.3 21.0 %all-to-all-start.4 = ((f32[64,1,4]{2,1,0:T(1,128)}), f32[64,1,4]{2,1,0:T(1,128)S(1)}, u32[]{:S(2)}, u32[]{:S(2)}) async-start(f32[64,1,4]{2,1,0:T(1,128)} %bitcast.30), calls=%async_computation.4 | async-start | bytes 65536 | tf_op jit(solution)/shard_map/all_to_all | solution.py:52
  22.5 3.9 copy-start.5
  28.3 43.3 %all-to-all-start.5 = ((f32[64,1,4]{2,1,0:T(1,128)}), f32[64,1,4]{2,1,0:T(1,128)S(1)}, u32[]{:S(2)}, u32[]{:S(2)}) async-start(f32[64,1,4]{2,1,0:T(1,128)} %bitcast.32), calls=%async_computation.5 | async-start | bytes 65536 | tf_op jit(solution)/shard_map/all_to_all | solution.py:59
  71.6 107.0 %all-to-all-start.6 = ((f32[64,4,4,1024]{3,2,1,0:T(4,128)}), f32[64,4,4,1024]{3,2,1,0:T(4,128)}, u32[]{:S(2)}, u32[]{:S(2)}) async-start(f32[64,4,4,1024]{3,2,1,0:T(4,128)} %bitcast.159), calls=%async_computation.6 | async-start | bytes 8388608 | tf_op jit(solution)/shard_map/all_to_all | solution.py:45
  178.6 34.4 %all-to-all-start.2 = ((f32[64,1,4]{2,1,0:T(1,128)}), f32[64,1,4]{2,1,0:T(1,128)S(1)}, u32[]{:S(2)}, u32[]{:S(2)}) async-start(f32[64,1,4]{2,1,0:T(1,128)} %bitcast.18), calls=%async_computation.2 | async-start | bytes 65536 | tf_op jit(solution)/shard_map/all_to_all | solution.py:52
  213.0 43.3 %all-to-all-start.3 = ((f32[64,1,4]{2,1,0:T(1,128)}), f32[64,1,4]{2,1,0:T(1,128)S(1)}, u32[]{:S(2)}, u32[]{:S(2)}) async-start(f32[64,1,4]{2,1,0:T(1,128)} %bitcast.20), calls=%async_computation.3 | async-start | bytes 65536 | tf_op jit(solution)/shard_map/all_to_all | solution.py:59
  256.3 107.1 %all-to-all-start.7 = ((f32[64,4,4,1024]{3,2,1,0:T(4,128)}), f32[64,4,4,1024]{3,2,1,0:T(4,128)}, u32[]{:S(2)}, u32[]{:S(2)}) async-start(f32[64,4,4,1024]{3,2,1,0:T(4,128)} %bitcast.160), calls=%async_computation.7 | async-start | bytes 8388608 | tf_op jit(solution)/shard_map/all_to_all | solution.py:45
  363.5 34.4 %all-to-all-start = ((f32[64,1,4]{2,1,0:T(1,128)}), f32[64,1,4]{2,1,0:T(1,128)S(1)}, u32[]{:S(2)}, u32[]{:S(2)}) async-start(f32[64,1,4]{2,1,0:T(1,128)} %bitcast.6), calls=%async_computation | async-start | bytes 65536 | tf_op jit(solution)/shard_map/all_to_all | solution.py:52
  397.9 43.3 %all-to-all-start.1 = ((f32[64,1,4]{2,1,0:T(1,128)}), f32[64,1,4]{2,1,0:T(1,128)S(1)}, u32[]{:S(2)}, u32[]{:S(2)}) async-start(f32[64,1,4]{2,1,0:T(1,128)} %bitcast.8), calls=%async_computation.1 | async-start | bytes 65536 | tf_op jit(solution)/shard_map/all_to_all | solution.py:59
  441.2 10.7 %copy-start.3 = (s32[4,8]{1,0:T(4,128)S(1)}, s32[4,8]{1,0:T(4,128)}, u32[]{:S(2)}) copy-start(s32[4,8]{1,0:T(4,128)} %param.11) | copy-start | bytes 388
  441.2 157.7 %copy-start.6 = (u32[256]{0:T(256)S(1)}, u32[256]{0:T(256)}, u32[]{:S(2)}) copy-start(u32[256]{0:T(256)} %constant.96) | copy-start | bytes 3076
  441.2 159.0 %copy-start.4 = (s32[1024]{0:T(1024)S(1)}, s32[1024]{0:T(1024)}, u32[]{:S(2)}) copy-start(s32[1024]{0:T(1024)} %param.10) | copy-start | bytes 12292
  441.2 160.3 %all-to-all-start.8 = ((f32[64,4,4,1024]{3,2,1,0:T(4,128)}), f32[64,4,4,1024]{3,2,1,0:T(4,128)}, u32[]{:S(2)}, u32[]{:S(2)}) async-start(f32[64,4,4,1024]{3,2,1,0:T(4,128)} %bitcast.161), calls=%async_computation.8 | async-start | bytes 8388608 | tf_op jit(solution)/shard_map/all_to_all | solution.py:45
  623.6 2.2 copy-start.2
  625.8 277.5 %copy-start.1 = (f32[64,4,1024]{2,1,0:T(4,128)S(1)}, f32[64,4,1024]{2,1,0:T(4,128)}, u32[]{:S(2)}) copy-start(f32[64,4,1024]{2,1,0:T(4,128)} %param.6) | copy-start | bytes 3145732
  639.7 260.6 %all-to-all-start.9 = ((f32[64,1,4]{2,1,0:T(1,128)}), f32[64,1,4]{2,1,0:T(1,128)S(1)}, u32[]{:S(2)}, u32[]{:S(2)}) async-start(f32[64,1,4]{2,1,0:T(1,128)} %bitcast.59), calls=%async_computation.9 | async-start | bytes 65536 | tf_op jit(solution)/shard_map/all_to_all | solution.py:96
where the time goes:
time: 914 us; the launch traced here: 904 us
  blocking collectives  397 us (43%)
  waiting for transfers between devices  182 us (20%)
  local copies, waits for them, and re-layouts  165 us (18%)
  starting transfers between devices  91.8 us (10%)
  other arithmetic  43.2 us (5%)
  matrix products  22.3 us (2%)
    unnamed x1, blocking collectives  251 us
    all_to_all x3, waiting for transfers between devices, on_device(): lax.all_to_all(buffer.reshape(owners, capacity, states, site_dev), 'node'...  182 us
    all_gather x1, blocking collectives, on_device(): incidence = lax.all_gather(topo_nodes, 'node', axis=0, tiled=True)  135 us
    scatter x3, local copies, waits for them, and re-layouts, on_device(): jnp.zeros((slots_all, states, site_dev), jnp.float32).at[slot_index]  78.5 us
    all_to_all x3, starting transfers between devices, on_device(): lax.all_to_all(buffer.reshape(owners, capacity, states, site_dev), 'node'...  32.3 us
    all_to_all x3, starting transfers between devices, on_device(): lax.all_to_all(weight_buffer.reshape(owners, capacity), 'node', split_axi...  30.9 us
    unnamed x21, local copies, waits for them, and re-layouts  26.9 us
    all_to_all x3, starting transfers between devices, on_device(): lax.all_to_all(code_buffer.reshape(owners, capacity), 'node', split_axis=...  20.7 us
  transfers between devices with their start and end apart: 10, of which 2 were waited for; matrix products, arithmetic and copies ran while one was open for 21% of the time, Pallas kernels for 0%

commit v1 on v0

--- a/solution.py
+++ b/solution.py
@@ -19,7 +19,9 @@
     nodes_all = node_dev * owners
     sites_all = site_dev * lax.axis_size("site")
     scaled = counts.astype(jnp.float32) / sites_all
-    incidence = lax.all_gather(topo_nodes, "node", axis=0, tiled=True)
+    incidence = jnp.concatenate(
+        lax.all_to_all(jnp.stack([topo_nodes] * lax.axis_size("node")), "node", 0, 0), axis=0
+    )
     multiplicity = jax.ops.segment_sum(
         jnp.ones((incidence.size,), jnp.float32), incidence.reshape(-1), num_segments=nodes_all
     )

time: 914 us -> 873 us (0.955)
  blocking collectives: 397 us -> 262 us
  waiting for transfers between devices: 182 us -> 273 us
    all_gather x1 -> x0, blocking collectives: 135 us -> none  [on_device(): incidence = lax.all_gather(topo_nodes, 'node', axis=0, tiled=True)]
    all_to_all x3, waiting for transfers between devices: 182 us -> 264 us  [on_device(): lax.all_to_all(buffer.reshape(owners, capacity, states, site_dev), 'node'...]
    all_to_all x3, waiting for transfers between devices: 0.01 us -> 9.48 us  [on_device(): lax.all_to_all(weight_buffer.reshape(owners, capacity), 'node', split_axi...]
  transfers between devices with their start and end apart: 10 -> 11, of which waited for: 2 -> 4; matrix products, arithmetic and copies ran while one was open for 21% -> 22% of each run, Pallas kernels for 0% -> 0%
where the time goes in v1:
time: 873 us; the launch traced here: 863 us
  waiting for transfers between devices  273 us (31%)
  blocking collectives  262 us (30%)
  local copies, waits for them, and re-layouts  166 us (19%)
  starting transfers between devices  94 us (11%)
  other arithmetic  43.2 us (5%)
  matrix products  22.3 us (3%)
    all_to_all x3, waiting for transfers between devices, on_device(): lax.all_to_all(buffer.reshape(owners, capacity, states, site_dev), 'node'...  264 us
    unnamed x1, blocking collectives  251 us
    scatter x3, local copies, waits for them, and re-layouts, on_device(): jnp.zeros((slots_all, states, site_dev), jnp.float32).at[slot_index]  78.5 us
    all_to_all x3, starting transfers between devices, on_device(): lax.all_to_all(buffer.reshape(owners, capacity, states, site_dev), 'node'...  32.6 us
    all_to_all x3, starting transfers between devices, on_device(): lax.all_to_all(weight_buffer.reshape(owners, capacity), 'node', split_axi...  30.9 us
    unnamed x21, local copies, waits for them, and re-layouts  26.9 us
    all_to_all x3, starting transfers between devices, on_device(): lax.all_to_all(code_buffer.reshape(owners, capacity), 'node', split_axis=...  20.7 us
    dot_general x3, matrix products, on_device(): jnp.dot(selector * received_weights.reshape(-1)[None, :], flat_rows, prec...  19.7 us
  transfers between devices with their start and end apart: 11, of which 4 were waited for; matrix products, arithmetic and copies ran while one was open for 22% of the time, Pallas kernels for 0%

profile of v1, /device:TPU:0, one launch (start us, length us, event | category | flops | bytes accessed | tf_op | source)
XLA Modules:
  0.0 862.6 jit_solution(13500582443958763485)
XLA Ops:
  0.6 0.9 fusion.54
  4.6 0.8 compare_select_fusion
  5.4 1.2 scatter_custom_fusion.4
  6.6 0.7 all_to_all.62
  7.3 10.2 %all-to-all-start.4 = ((f32[64,1,4]{2,1,0:T(1,128)}), f32[64,1,4]{2,1,0:T(1,128)S(1)}, u32[]{:S(2)}, u32[]{:S(2)}) async-start(f32[64,1,4]{2,1,0:T(1,128)} %bitcast.30), calls=%async_computation.4 | async-start | bytes 65536 | tf_op jit(solution)/shard_map/all_to_all | solution.py:54
  17.6 0.8 multiply_exponential_fusion.2
  18.4 4.1 gather_fusion
  22.5 3.8 reduce_sum.102
  26.4 1.2 scatter_custom_fusion.5
  27.6 0.7 all_to_all.64
  28.3 10.3 %all-to-all-start.5 = ((f32[64,1,4]{2,1,0:T(1,128)}), f32[64,1,4]{2,1,0:T(1,128)S(1)}, u32[]{:S(2)}, u32[]{:S(2)}) async-start(f32[64,1,4]{2,1,0:T(1,128)} %bitcast.32), calls=%async_computation.5 | async-start | bytes 65536 | tf_op jit(solution)/shard_map/all_to_all | solution.py:61
  38.6 3.8 multiply_add_fusion.2
  42.4 3.0 broadcast.596.clone.1
  45.5 26.2 %scatter_fusion = f32[256,4,1024]{2,1,0:T(4,128)} fusion(f32[256,4,1024]{2,1,0:T(4,128)} %broadcast.596.clone.1, s32[192]{0:T(256)S(1)} %bitcast.184, f32[192,4,1024]{2,1,0:T(4,128)} %multiply_add_fusion.2), kind=kCustom, calls=%fused_computation.11 | custom fusion | bytes 9437952 | tf_op jit(solution)/shard_map/scatter | solution.py:41
  71.6 10.7 %all-to-all-start.6 = ((f32[64,4,4,1024]{3,2,1,0:T(4,128)}), f32[64,4,4,1024]{3,2,1,0:T(4,128)}, u32[]{:S(2)}, u32[]{:S(2)}) async-start(f32[64,4,4,1024]{3,2,1,0:T(4,128)} %bitcast.158), calls=%async_computation.6 | async-start | bytes 8388608 | tf_op jit(solution)/shard_map/all_to_all | solution.py:47
  82.4 1.2 scatter_custom_fusion.2
  83.6 0.7 all_to_all.58
  84.3 1.2 scatter_custom_fusion.3
  86.9 0.7 reduce.35
  87.8 90.8 %all-to-all-done.6 = f32[64,4,4,1024]{3,2,1,0:T(4,128)} async-done(((f32[64,4,4,1024]{3,2,1,0:T(4,128)}), f32[64,4,4,1024]{3,2,1,0:T(4,128)}, u32[]{:S(2)}, u32[]{:S(2)}) %all-to-all-start.6) | async-done | bytes 4194336 | tf_op jit(solution)/shard_map/all_to_all | solution.py:47
  178.6 5.3 all-to-all-start.2
  183.8 8.0 copy.51
  191.8 5.8 copy.35
  197.6 6.6 fusion.4
  205.0 4.1 gather_fusion.1
  209.1 3.8 reduce_sum.103
  213.0 10.3 %all-to-all-start.3 = ((f32[64,1,4]{2,1,0:T(1,128)}), f32[64,1,4]{2,1,0:T(1,128)S(1)}, u32[]{:S(2)}, u32[]{:S(2)}) async-start(f32[64,1,4]{2,1,0:T(1,128)} %bitcast.20), calls=%async_computation.3 | async-start | bytes 65536 | tf_op jit(solution)/shard_map/all_to_all | solution.py:61
  223.3 3.8 multiply_add_fusion.1
  227.1 3.0 broadcast.596.clone
  230.1 26.2 %scatter_fusion.1 = f32[256,4,1024]{2,1,0:T(4,128)} fusion(f32[256,4,1024]{2,1,0:T(4,128)} %broadcast.596.clone, s32[192]{0:T(256)S(1)} %bitcast.180, f32[192,4,1024]{2,1,0:T(4,128)} %multiply_add_fusion.1), kind=kCustom, calls=%fused_computation.12 | custom fusion | bytes 9437952 | tf_op jit(solution)/shard_map/scatter | solution.py:41
  256.3 10.9 %all-to-all-start.7 = ((f32[64,4,4,1024]{3,2,1,0:T(4,128)}), f32[64,4,4,1024]{3,2,1,0:T(4,128)}, u32[]{:S(2)}, u32[]{:S(2)}) async-start(f32[64,4,4,1024]{3,2,1,0:T(4,128)} %bitcast.159), calls=%async_computation.7 | async-start | bytes 8388608 | tf_op jit(solution)/shard_map/all_to_all | solution.py:47
  267.3 1.2 scatter_custom_fusion
  268.5 0.7 all_to_all.54
  269.2 1.2 scatter_custom_fusion.1
  271.3 0.7 reduce.36
  272.2 91.3 %all-to-all-done.7 = f32[64,4,4,1024]{3,2,1,0:T(4,128)} async-done(((f32[64,4,4,1024]{3,2,1,0:T(4,128)}), f32[64,4,4,1024]{3,2,1,0:T(4,128)}, u32[]{:S(2)}, u32[]{:S(2)}) %all-to-all-start.7) | async-done | bytes 4194336 | tf_op jit(solution)/shard_map/all_to_all | solution.py:47
  363.5 5.3 all-to-all-start
  368.7 8.0 copy.52
  376.7 5.7 copy.37
  382.4 6.6 fusion.6
  389.9 4.1 gather_fusion.2
  394.0 3.8 reduce_sum.104
  397.8 10.3 %all-to-all-start.1 = ((f32[64,1,4]{2,1,0:T(1,128)}), f32[64,1,4]{2,1,0:T(1,128)S(1)}, u32[]{:S(2)}, u32[]{:S(2)}) async-start(f32[64,1,4]{2,1,0:T(1,128)} %bitcast.8), calls=%async_computation.1 | async-start | bytes 65536 | tf_op jit(solution)/shard_map/all_to_all | solution.py:61
  408.2 9.5 %all-to-all-done.1 = f32[64,1,4]{2,1,0:T(1,128)S(1)} async-done(((f32[64,1,4]{2,1,0:T(1,128)}), f32[64,1,4]{2,1,0:T(1,128)S(1)}, u32[]{:S(2)}, u32[]{:S(2)}) %all-to-all-start.1) | async-done | bytes 1056 | tf_op jit(solution)/shard_map/all_to_all | solution.py:61
  418.4 4.6 all-to-all-start.9
  423.0 3.8 multiply_add_fusion
  426.8 3.0 broadcast.596
  429.8 26.2 %scatter_fusion.2 = f32[256,4,1024]{2,1,0:T(4,128)} fusion(f32[256,4,1024]{2,1,0:T(4,128)} %broadcast.596, s32[192]{0:T(256)S(1)} %bitcast.170, f32[192,4,1024]{2,1,0:T(4,128)} %multiply_add_fusion), kind=kCustom, calls=%fused_computation.13 | custom fusion | bytes 9437952 | tf_op jit(solution)/shard_map/scatter | solution.py:41
  456.0 10.9 %all-to-all-start.8 = ((f32[64,4,4,1024]{3,2,1,0:T(4,128)}), f32[64,4,4,1024]{3,2,1,0:T(4,128)}, u32[]{:S(2)}, u32[]{:S(2)}) async-start(f32[64,4,4,1024]{3,2,1,0:T(4,128)} %bitcast.160), calls=%async_computation.8 | async-start | bytes 8388608 | tf_op jit(solution)/shard_map/all_to_all | solution.py:47
  468.5 0.7 reduce.37
  469.5 11.2 %scatter_custom_fusion.9 = f32[4096]{0:T(1024)S(1)} fusion(s32[2048]{0:T(1024)S(1)} %reshape.802, f32[2048]{0:T(1024)S(1)} %broadcast.602, f32[]{:T(128)} %constant.79.clone.1), kind=kCustom, calls=%fused_computation.94 | custom fusion | flops 2048 | bytes 16388 | tf_op jit(solution)/shard_map/scatter-add | solution.py:25
  481.2 81.9 %all-to-all-done.8 = f32[64,4,4,1024]{3,2,1,0:T(4,128)} async-done(((f32[64,4,4,1024]{3,2,1,0:T(4,128)}), f32[64,4,4,1024]{3,2,1,0:T(4,128)}, u32[]{:S(2)}, u32[]{:S(2)}) %all-to-all-start.8) | async-done | bytes 4194336 | tf_op jit(solution)/shard_map/all_to_all | solution.py:47
  563.1 7.9 copy.53
  571.0 5.6 copy.39
  576.6 6.6 fusion.8
  583.8 1.4 copy.40
  585.2 1.7 copy.54
  587.4 2.4 fusion
  589.8 10.7 %all-reduce.4 = (f32[64]{0:T(128)S(1)}, f32[256]{0:T(256)S(1)}) all-reduce(f32[64]{0:T(128)S(1)} %get-tuple-element.11, f32[256]{0:T(256)S(1)} %fusion), channel_id=1, replica_groups=mesh['node'=64,'site'=4] {'site'}, use_global_device_ids=true, to_apply=%region_23.24 | all-reduce | flops 320 | bytes 2560 | tf_op jit(solution)/shard_map/psum | solution.py:92
  600.6 0.7 all_to_all.70
  601.3 5.2 all-to-all-start.10
  606.8 251.0 %all-reduce.3 = f32[4096]{0:T(1024)S(1)} all-reduce(f32[4096]{0:T(1024)S(1)} %dynamic-update-slice), channel_id=1, replica_groups=mesh['node'=64,'site'=4] {'node'}, use_global_device_ids=true, to_apply=%add.3 | all-reduce | flops 4096 | bytes 32768
  859.2 0.7 reduce.38
  860.1 2.2 gather_fusion.4
  (98 shorter events, 12.9 us)
Async XLA Ops:
  0.6 17.8 %copy-start = (f32[64,4,1024]{2,1,0:T(4,128)S(1)}, f32[64,4,1024]{2,1,0:T(4,128)}, u32[]{:S(2)}) copy-start(f32[64,4,1024]{2,1,0:T(4,128)} %param.6) | copy-start | bytes 3145732
  7.3 21.0 %all-to-all-start.4 = ((f32[64,1,4]{2,1,0:T(1,128)}), f32[64,1,4]{2,1,0:T(1,128)S(1)}, u32[]{:S(2)}, u32[]{:S(2)}) async-start(f32[64,1,4]{2,1,0:T(1,128)} %bitcast.30), calls=%async_computation.4 | async-start | bytes 65536 | tf_op jit(solution)/shard_map/all_to_all | solution.py:54
  22.5 3.9 copy-start.5
  28.3 43.3 %all-to-all-start.5 = ((f32[64,1,4]{2,1,0:T(1,128)}), f32[64,1,4]{2,1,0:T(1,128)S(1)}, u32[]{:S(2)}, u32[]{:S(2)}) async-start(f32[64,1,4]{2,1,0:T(1,128)} %bitcast.32), calls=%async_computation.5 | async-start | bytes 65536 | tf_op jit(solution)/shard_map/all_to_all | solution.py:61
  71.6 107.0 %all-to-all-start.6 = ((f32[64,4,4,1024]{3,2,1,0:T(4,128)}), f32[64,4,4,1024]{3,2,1,0:T(4,128)}, u32[]{:S(2)}, u32[]{:S(2)}) async-start(f32[64,4,4,1024]{3,2,1,0:T(4,128)} %bitcast.158), calls=%async_computation.6 | async-start | bytes 8388608 | tf_op jit(solution)/shard_map/all_to_all | solution.py:47
  178.6 34.4 %all-to-all-start.2 = ((f32[64,1,4]{2,1,0:T(1,128)}), f32[64,1,4]{2,1,0:T(1,128)S(1)}, u32[]{:S(2)}, u32[]{:S(2)}) async-start(f32[64,1,4]{2,1,0:T(1,128)} %bitcast.18), calls=%async_computation.2 | async-start | bytes 65536 | tf_op jit(solution)/shard_map/all_to_all | solution.py:54
  213.0 43.3 %all-to-all-start.3 = ((f32[64,1,4]{2,1,0:T(1,128)}), f32[64,1,4]{2,1,0:T(1,128)S(1)}, u32[]{:S(2)}, u32[]{:S(2)}) async-start(f32[64,1,4]{2,1,0:T(1,128)} %bitcast.20), calls=%async_computation.3 | async-start | bytes 65536 | tf_op jit(solution)/shard_map/all_to_all | solution.py:61
  256.3 107.1 %all-to-all-start.7 = ((f32[64,4,4,1024]{3,2,1,0:T(4,128)}), f32[64,4,4,1024]{3,2,1,0:T(4,128)}, u32[]{:S(2)}, u32[]{:S(2)}) async-start(f32[64,4,4,1024]{3,2,1,0:T(4,128)} %bitcast.159), calls=%async_computation.7 | async-start | bytes 8388608 | tf_op jit(solution)/shard_map/all_to_all | solution.py:47
  363.5 34.3 %all-to-all-start = ((f32[64,1,4]{2,1,0:T(1,128)}), f32[64,1,4]{2,1,0:T(1,128)S(1)}, u32[]{:S(2)}, u32[]{:S(2)}) async-start(f32[64,1,4]{2,1,0:T(1,128)} %bitcast.6), calls=%async_computation | async-start | bytes 65536 | tf_op jit(solution)/shard_map/all_to_all | solution.py:54
  393.9 23.7 %copy-start.3 = (s32[4,8]{1,0:T(4,128)S(1)}, s32[4,8]{1,0:T(4,128)}, u32[]{:S(2)}) copy-start(s32[4,8]{1,0:T(4,128)} %param.11) | copy-start | bytes 388
  397.8 19.9 %all-to-all-start.1 = ((f32[64,1,4]{2,1,0:T(1,128)}), f32[64,1,4]{2,1,0:T(1,128)S(1)}, u32[]{:S(2)}, u32[]{:S(2)}) async-start(f32[64,1,4]{2,1,0:T(1,128)} %bitcast.8), calls=%async_computation.1 | async-start | bytes 65536 | tf_op jit(solution)/shard_map/all_to_all | solution.py:61
  418.4 37.6 %all-to-all-start.9 = ((s32[64,4,8]{2,1,0:T(4,128)}), s32[64,4,8]{2,1,0:T(4,128)S(1)}, u32[]{:S(2)}, u32[]{:S(2)}) async-start(s32[64,4,8]{2,1,0:T(4,128)} %stack.2), calls=%async_computation.9 | async-start | bytes 262144 | tf_op jit(solution)/shard_map/all_to_all | solution.py:23
  456.0 11.0 %copy-start.6 = (u32[256]{0:T(256)S(1)}, u32[256]{0:T(256)}, u32[]{:S(2)}) copy-start(u32[256]{0:T(256)} %constant.96) | copy-start | bytes 3076
  456.0 12.3 %copy-start.4 = (s32[1024]{0:T(1024)S(1)}, s32[1024]{0:T(1024)}, u32[]{:S(2)}) copy-start(s32[1024]{0:T(1024)} %param.10) | copy-start | bytes 12292
  456.0 107.1 %all-to-all-start.8 = ((f32[64,4,4,1024]{3,2,1,0:T(4,128)}), f32[64,4,4,1024]{3,2,1,0:T(4,128)}, u32[]{:S(2)}, u32[]{:S(2)}) async-start(f32[64,4,4,1024]{3,2,1,0:T(4,128)} %bitcast.160), calls=%async_computation.8 | async-start | bytes 8388608 | tf_op jit(solution)/shard_map/all_to_all | solution.py:47
  585.2 2.2 copy-start.2
  587.4 274.9 %copy-start.1 = (f32[64,4,1024]{2,1,0:T(4,128)S(1)}, f32[64,4,1024]{2,1,0:T(4,128)}, u32[]{:S(2)}) copy-start(f32[64,4,1024]{2,1,0:T(4,128)} %param.6) | copy-start | bytes 3145732
  601.3 258.0 %all-to-all-start.10 = ((f32[64,1,4]{2,1,0:T(1,128)}), f32[64,1,4]{2,1,0:T(1,128)S(1)}, u32[]{:S(2)}, u32[]{:S(2)}) async-start(f32[64,1,4]{2,1,0:T(1,128)} %bitcast.58), calls=%async_computation.10 | async-start | bytes 65536 | tf_op jit(solution)/shard_map/all_to_all | solution.py:98
